TPU v7x, 32 devices: a whole 2x2x4 slice. The times are simulated.
32 devices in a mesh: seq: 8 (over y, x, core), head: 4 (over z).
Axes of the slice: x: 2, y: 2, z: 4, core: 2. Of those that a mesh axis runs over, the one named last changes fastest.
Arguments:
- query_lin: bfloat16 [512, 4096], P('seq', 'head'), may hold values from -6 to 6
- key_lin: bfloat16 [512, 4096], P('seq', 'head'), may hold values from -6 to 6
- value_lin: bfloat16 [512, 4096], P('seq', 'head'), may hold values from -6 to 6
- log_decay: float32 [32, 512], P('head', 'seq'), may hold values from -1.6 to 0
- query_soft: bfloat16 [512, 4096], P(('seq', 'head')), may hold values from -4.5 to 4.5
- key_soft: bfloat16 [512, 512], P(('seq', 'head')), may hold values from -4.5 to 4.5
- value_soft: bfloat16 [512, 512], P(('seq', 'head')), may hold values from -6 to 6
- doc_start: int32 [512], P('seq'), may hold values from 0 to 480, as said below
Outputs:
- lin_out: bfloat16 [512, 4096], P('seq', 'head')
- soft_out: bfloat16 [512, 4096], P('seq', 'head')
- soft_lse: float32 [32, 512], P('head', 'seq')
Inputs may be any that keep to these rules, and one draw needn't show every extreme that they name: doc_start[t] is the first position of the document that holds token t: 0 for the first document, never above t, the same over a document; at most 4 documents; every document but the first and the last starts at a position of 1 to 32; the last document starts at 480.
All inputs are finite; a program needn't handle non-finite values.
Results may differ from a plain program's by a relative error of at most 0.003.
Values may be sent and summed in bfloat16 or wider, within the bound.
A program may use at most 256 MiB of HBM per device.

v0:
```python
import jax
import jax.numpy as jnp
from jax import lax
from jax.sharding import PartitionSpec as P

DH = 128
HIGHEST = lax.Precision.HIGHEST
masked_score = -1e30


def prefix(array, axis, combine, identity):
    size, here = (lax.axis_size(axis), lax.axis_index(axis))
    everything = jax.tree.map(lambda part: lax.all_gather(part, axis), array)
    start = jax.tree.map(
        lambda part, zero: jnp.broadcast_to(jnp.asarray(zero, part.dtype), part.shape),
        array,
        identity,
    )

    def lap(k, before):
        reached = k < here
        new = combine(before, jax.tree.map(lambda part: part[k], everything))
        return jax.tree.map(lambda a, b: jnp.where(reached, a, b), new, before)

    return lax.fori_loop(0, size, lap, start)


def span_terms(query_heads, key_heads, value_heads, decay_rows, doc_rows, first_place):
    span_len = query_heads.shape[0]
    cumulative = jnp.cumsum(decay_rows, axis=1)
    totals = cumulative[:, -1]
    token_positions = first_place + jnp.arange(span_len, dtype=jnp.int32)
    allowed = (token_positions[None, :] <= token_positions[:, None]) & (
        doc_rows[:, None] <= token_positions[None, :]
    )
    decay_gap = jnp.where(allowed[None], cumulative[:, :, None] - cumulative[:, None, :], 0.0)
    decay_mat = jnp.where(allowed[None], jnp.exp(decay_gap), 0.0)
    scores = jnp.einsum("thd,shd->hts", query_heads, key_heads, preferred_element_type=jnp.float32)
    key_float = key_heads.astype(jnp.float32)
    value_float = value_heads.astype(jnp.float32)
    inner_part = jnp.einsum("hts,shd->thd", scores * decay_mat, value_float, precision=HIGHEST)
    keep_mask = (doc_rows == doc_rows[-1]).astype(jnp.float32)
    tail_weight = jnp.exp(totals[:, None] - cumulative) * keep_mask[None, :]
    weighted_keys = key_float * jnp.transpose(tail_weight)[:, :, None]
    fresh_state = jnp.einsum("shd,she->hde", weighted_keys, value_float, precision=HIGHEST)
    carry_on = (doc_rows[-1] < first_place).astype(jnp.float32)
    factor = jnp.exp(totals) * carry_on
    read_mask = (doc_rows < first_place).astype(jnp.float32)[:, None] * jnp.transpose(
        jnp.exp(cumulative)
    )
    return (inner_part, fresh_state, factor, read_mask)


def combine_states(earlier, later_part):
    return (earlier[0] * later_part[0], later_part[0][:, None, None] * earlier[1] + later_part[1])


def lightning_part(query_lin, key_lin, value_lin, log_decay, doc_start):
    span_len = query_lin.shape[0]
    head_count = log_decay.shape[0]
    first_place = lax.axis_index("seq") * span_len
    query_heads = query_lin.reshape(span_len, head_count, DH)
    key_heads = key_lin.reshape(span_len, head_count, DH)
    value_heads = value_lin.reshape(span_len, head_count, DH)
    inner_part, fresh_state, factor, read_mask = span_terms(
        query_heads, key_heads, value_heads, log_decay, doc_start, first_place
    )
    identity = (jnp.ones((head_count,), jnp.float32), jnp.zeros((head_count, DH, DH), jnp.float32))
    unused, carried = prefix((factor, fresh_state), "seq", combine_states, identity)
    outer_part = (
        jnp.einsum("thd,hde->the", query_heads.astype(jnp.float32), carried, precision=HIGHEST)
        * read_mask[:, :, None]
    )
    mixed_out = inner_part + outer_part
    normed = mixed_out * lax.rsqrt(jnp.mean(mixed_out * mixed_out, axis=-1, keepdims=True) + 1e-06)
    return normed.astype(jnp.bfloat16).reshape(span_len, head_count * DH)


def softmax_part(query_soft, key_soft, value_soft, doc_start):
    queries, keys_local, values_local = (
        lax.all_to_all(query_soft, "head", split_axis=1, concat_axis=0, tiled=True),
        lax.all_to_all(key_soft, "head", split_axis=1, concat_axis=0, tiled=True),
        lax.all_to_all(value_soft, "head", split_axis=1, concat_axis=0, tiled=True),
    )
    span_len = queries.shape[0]
    kv_count = keys_local.shape[1] // DH
    group_size = queries.shape[1] // keys_local.shape[1]
    first_place = lax.axis_index("seq") * span_len
    query_places = first_place + jnp.arange(span_len, dtype=jnp.int32)
    query_heads = queries.reshape(span_len, kv_count, group_size, DH)
    score_scale = DH ** (-0.5)
    start_state = (
        jnp.full((span_len, kv_count, group_size), masked_score, jnp.float32),
        jnp.zeros((span_len, kv_count, group_size), jnp.float32),
        jnp.zeros((span_len, kv_count, group_size, DH), jnp.float32),
    )
    key_piece = lax.all_gather(keys_local, "seq", axis=0, tiled=True)
    value_piece = lax.all_gather(values_local, "seq", axis=0, tiled=True)
    piece_rows = key_piece.shape[0]
    block_rows = max(
        (divisor for divisor in range(1, min(piece_rows, 1024) + 1) if piece_rows % divisor == 0)
    )
    block_count = piece_rows // block_rows
    key_parts = key_piece.reshape(block_count, block_rows, kv_count, DH)
    value_parts = value_piece.reshape(block_count, block_rows, kv_count, DH)
    begin_rows = jnp.int32(0) + block_rows * jnp.arange(block_count, dtype=jnp.int32)

    def absorb_block(running, slices):
        key_block, value_block, begin_row = slices
        running_max, norm_sum, accum_out = running
        token_positions = begin_row + jnp.arange(block_rows, dtype=jnp.int32)
        allowed = (token_positions[None, :] <= query_places[:, None]) & (
            doc_start[:, None] <= token_positions[None, :]
        )
        allowed = allowed[:, None, None, :]
        scores = (
            jnp.einsum("tkgd,skd->tkgs", query_heads, key_block, preferred_element_type=jnp.float32)
            * score_scale
        )
        new_max = jnp.maximum(
            running_max, jnp.max(jnp.where(allowed, scores, masked_score), axis=-1)
        )
        raw_weight = jnp.where(allowed, jnp.exp(scores - new_max[..., None]), 0.0)
        shrink = jnp.exp(running_max - new_max)
        norm_sum = norm_sum * shrink + jnp.sum(raw_weight, axis=-1)
        accum_out = accum_out * shrink[..., None] + jnp.einsum(
            "tkgs,skd->tkgd",
            raw_weight.astype(jnp.bfloat16),
            value_block,
            preferred_element_type=jnp.float32,
        )
        running = (new_max, norm_sum, accum_out)
        return (running, None)

    final_state, unused = lax.scan(absorb_block, start_state, (key_parts, value_parts, begin_rows))
    running_max, norm_sum, accum_out = final_state
    soft_out = (
        (accum_out / norm_sum[..., None])
        .astype(jnp.bfloat16)
        .reshape(span_len, kv_count * group_size * DH)
    )
    soft_lse = jnp.transpose(
        (running_max + jnp.log(norm_sum)).reshape(span_len, kv_count * group_size)
    )
    return (soft_out, soft_lse)


def per_device(
    query_lin, key_lin, value_lin, log_decay, query_soft, key_soft, value_soft, doc_start
):
    lin_out = lightning_part(query_lin, key_lin, value_lin, log_decay, doc_start)
    soft_out, soft_lse = softmax_part(query_soft, key_soft, value_soft, doc_start)
    return (lin_out, soft_out, soft_lse)


def solution(mesh):
    return jax.shard_map(
        per_device,
        mesh=mesh,
        in_specs=(
            P("seq", "head"),
            P("seq", "head"),
            P("seq", "head"),
            P("head", "seq"),
            P(("seq", "head"), None),
            P(("seq", "head"), None),
            P(("seq", "head"), None),
            P("seq"),
        ),
        out_specs=(P("seq", "head"), P("seq", "head"), P("head", "seq")),
        check_vma=False,
    )
```

profile of v0, /device:TPU:0, one launch (start us, length us, event | category | flops | bytes accessed | tf_op | source)
XLA Modules:
  0.0 91.8 jit_solution(14963114871208304785)
XLA Ops:
  7.2 1.2 %slice.8 = s32[1]{0:T(128)} slice(s32[64]{0:T(128)} %param.17), slice={[63:64]} | slice | bytes 8 | tf_op jit(solution)/shard_map/slice | solution.py:46
  9.1 1.3 %compare_convert_fusion = (f32[64]{0:T(128)S(1)}, f32[64]{0:T(128)S(1)}) fusion(s32[64]{0:T(128)} %param.17, s32[]{:T(128)S(6)} %mul.138, s32[]{:T(128)} %bitcast.1), kind=kLoop, calls=%fused_computation.64 | loop fusion | flops 256 | bytes 776 | tf_op jit(solution)/shard_map/convert_element_type | solution.py:48
  11.6 2.4 %fusion.11 = f32[8,128,128]{2,1,0:T(8,128)} fusion(f32[64,8]{0,1:T(8,128)S(1)} %get-tuple-element.160, bf16[64,1024]{1,0:T(8,128)(2,1)S(1)} %copy-done, bf16[64,1024]{1,0:T(8,128)(2,1)} %param.11), kind=kOutput, calls=%fused_computation.22 | convolution fusion | flops 100794368 | bytes 788480 | tf_op jit(solution)/shard_map/shd,she->hde/dot_general | solution.py:45
  14.0 1.3 %copy_bitcast_fusion.4 = bf16[16,4,128]{2,0,1:T(8,128)(2,1)} fusion(bf16[16,512]{1,0:T(8,128)(2,1)} %param.15), kind=kLoop, calls=%fused_computation.50 | loop fusion | bytes 32768 | tf_op jit(solution)/shard_map/all_to_all | solution.py:82
  15.3 6.3 %all-to-all-start = ((bf16[16,4,128]{2,0,1:T(8,128)(2,1)}), bf16[16,4,128]{2,0,1:T(8,128)(2,1)S(1)}, u32[]{:S(2)}, u32[]{:S(2)}) async-start(bf16[16,4,128]{2,0,1:T(8,128)(2,1)} %copy_bitcast_fusion.4), calls=%async_computation | async-start | bytes 32768 | tf_op jit(solution)/shard_map/all_to_all | solution.py:82
  21.7 1.3 %copy_bitcast_fusion.3 = bf16[16,4,128]{2,0,1:T(8,128)(2,1)} fusion(bf16[16,512]{1,0:T(8,128)(2,1)} %param.16), kind=kLoop, calls=%fused_computation.49 | loop fusion | bytes 32768 | tf_op jit(solution)/shard_map/all_to_all | solution.py:83
  23.7 3.5 %all-to-all-done = bf16[16,4,128]{2,0,1:T(8,128)(2,1)S(1)} async-done(((bf16[16,4,128]{2,0,1:T(8,128)(2,1)}), bf16[16,4,128]{2,0,1:T(8,128)(2,1)S(1)}, u32[]{:S(2)}, u32[]{:S(2)}) %all-to-all-start) | async-done | bytes 16416 | tf_op jit(solution)/shard_map/all_to_all | solution.py:82
  27.3 3.3 %all-to-all-start.2 = ((bf16[16,4,128]{2,0,1:T(8,128)(2,1)}), bf16[16,4,128]{2,0,1:T(8,128)(2,1)S(1)}, u32[]{:S(2)}, u32[]{:S(2)}) async-start(bf16[16,4,128]{2,0,1:T(8,128)(2,1)} %copy_bitcast_fusion.3), calls=%async_computation.2 | async-start | bytes 32768 | tf_op jit(solution)/shard_map/all_to_all | solution.py:83
  30.5 1.2 %convolution_multiply_fusion.1 = f32[8,64,64]{2,1,0:T(8,128)S(1)} fusion(f32[8,64]{1,0:T(8,128)S(1)} %reduce_window_sum.11, pred[64,64]{1,0:T(8,128)(4,1)S(1)} %compare_and_fusion, bf16[64,1024]{1,0:T(8,128)(2,1)} %param.11, bf16[64,1024]{1,0:T(8,128)(2,1)} %param.10), kind=kOutput, calls=%fused_computation.10 | convolution fusion | flops 8519680 | bytes 399360 | tf_op jit(solution)/shard_map/thd,shd->hts/dot_general | solution.py:38
  31.7 1.2 %dynamic-slice = u32[1]{0:T(128)} dynamic-slice(u32[32]{0:T(128)} %constant.72, u32[]{:T(128)S(6)} %add.102), dynamic_slice_sizes={1} | dynamic-slice | bytes 12
  33.9 12.5 %all-reduce = f32[64]{0:T(128)S(1)} all-reduce(f32[64]{0:T(128)S(1)} %dynamic-update-slice), channel_id=2, replica_groups=mesh['seq'=8,'head'=4] {'seq'}, use_global_device_ids=true, to_apply=%add | all-reduce | flops 64 | bytes 512
  46.5 1.6 %copy.93 = bf16[2,4,8,1024]{3,2,0,1:T(8,128)(2,1)} copy(bf16[2,4,8,1024]{3,2,1,0:T(8,128)(2,1)} %bitcast.145) | data formatting | bytes 262144 | tf_op jit(solution)/shard_map/all_to_all | solution.py:81
  48.1 4.8 %all-to-all-start.1 = ((bf16[16,4,1024]{2,0,1:T(8,128)(2,1)}), bf16[16,4,1024]{2,0,1:T(8,128)(2,1)S(1)}, u32[]{:S(2)}, u32[]{:S(2)}) async-start(bf16[16,4,1024]{2,0,1:T(8,128)(2,1)} %bitcast.137), calls=%async_computation.1 | async-start | bytes 262144 | tf_op jit(solution)/shard_map/all_to_all | solution.py:81
  53.6 9.1 %all_gather.19 = bf16[512,128]{1,0:T(8,128)(2,1)S(1)} all-gather(bf16[64,128]{1,0:T(8,128)(2,1)S(1)} %bitcast.148), channel_id=1, replica_groups=mesh['seq'=8,'head'=4] {'seq'}, dimensions={0}, use_global_device_ids=true | all-gather | bytes 147456 | tf_op jit(solution)/shard_map/all_gather | solution.py:97
  62.7 8.4 %all_gather.20 = bf16[512,128]{1,0:T(8,128)(2,1)S(1)} all-gather(bf16[64,128]{1,0:T(8,128)(2,1)S(1)} %bitcast.149), channel_id=1, replica_groups=mesh['seq'=8,'head'=4] {'seq'}, dimensions={0}, use_global_device_ids=true | all-gather | bytes 147456 | tf_op jit(solution)/shard_map/all_gather | solution.py:98
  73.8 9.7 %while.9 = (s32[]{:T(128)}, f32[8,128,128]{2,1,0:T(8,128)S(1)}, s32[]{:T(128)}, f32[8,8]{1,0:T(8,128)S(1)}, f32[8,8,128,128]{3,2,1,0:T(8,128)}, /*index=5*/s32[]{:T(128)}, s32[]{:T(128)}) while((s32[]{:T(128)}, f32[8,128,128]{2,1,0:T(8,128)S(1)}, s32[]{:T(128)}, f32[8,8]{1,0:T(8,128)S(1)}, f32[8,8,128,128]{3,2,1,0:T(8,128)}, ...), condition=%wide.region_2.3_spmd.clone, body=%wide.region_1.2_spmd.clone.sunk | while | flops 524292 | bytes 1573065 | solution.py:25
  73.8 1.2 %fusion.49 = f32[8,128,128]{2,1,0:T(8,128)S(1)} fusion(f32[8,8,128,128]{3,2,1,0:T(8,128)} %get-tuple-element.216, s32[]{:T(128)} %get-tuple-element.205, f32[8,128,128]{2,1,0:T(8,128)S(1)} %get-tuple-element.206, f32[8]{0:T(128)S(1)} %dynamic-slice_bitcast_fusion.2, pred[]{:T(512)S(6)} %compare.3, pred[]{:T(512)S(6)} %lt.33), kind=kLoop, calls=%fused_computation.1.clone.1 | loop fusion | flops 524288 | bytes 1572902 | tf_op jit(solution)/shard_map/while/body/eval_jaxpr/jit(_where)/select_n | solution.py:23
  75.0 1.2 %fusion.49 = f32[8,128,128]{2,1,0:T(8,128)S(1)} fusion(f32[8,8,128,128]{3,2,1,0:T(8,128)} %get-tuple-element.216, s32[]{:T(128)} %get-tuple-element.205, f32[8,128,128]{2,1,0:T(8,128)S(1)} %get-tuple-element.206, f32[8]{0:T(128)S(1)} %dynamic-slice_bitcast_fusion.2, pred[]{:T(512)S(6)} %compare.3, pred[]{:T(512)S(6)} %lt.33), kind=kLoop, calls=%fused_computation.1.clone.1 | loop fusion | flops 524288 | bytes 1572902 | tf_op jit(solution)/shard_map/while/body/eval_jaxpr/jit(_where)/select_n | solution.py:23
  76.2 1.2 %fusion.49 = f32[8,128,128]{2,1,0:T(8,128)S(1)} fusion(f32[8,8,128,128]{3,2,1,0:T(8,128)} %get-tuple-element.216, s32[]{:T(128)} %get-tuple-element.205, f32[8,128,128]{2,1,0:T(8,128)S(1)} %get-tuple-element.206, f32[8]{0:T(128)S(1)} %dynamic-slice_bitcast_fusion.2, pred[]{:T(512)S(6)} %compare.3, pred[]{:T(512)S(6)} %lt.33), kind=kLoop, calls=%fused_computation.1.clone.1 | loop fusion | flops 524288 | bytes 1572902 | tf_op jit(solution)/shard_map/while/body/eval_jaxpr/jit(_where)/select_n | solution.py:23
  77.4 1.2 %fusion.49 = f32[8,128,128]{2,1,0:T(8,128)S(1)} fusion(f32[8,8,128,128]{3,2,1,0:T(8,128)} %get-tuple-element.216, s32[]{:T(128)} %get-tuple-element.205, f32[8,128,128]{2,1,0:T(8,128)S(1)} %get-tuple-element.206, f32[8]{0:T(128)S(1)} %dynamic-slice_bitcast_fusion.2, pred[]{:T(512)S(6)} %compare.3, pred[]{:T(512)S(6)} %lt.33), kind=kLoop, calls=%fused_computation.1.clone.1 | loop fusion | flops 524288 | bytes 1572902 | tf_op jit(solution)/shard_map/while/body/eval_jaxpr/jit(_where)/select_n | solution.py:23
  78.6 1.2 %fusion.49 = f32[8,128,128]{2,1,0:T(8,128)S(1)} fusion(f32[8,8,128,128]{3,2,1,0:T(8,128)} %get-tuple-element.216, s32[]{:T(128)} %get-tuple-element.205, f32[8,128,128]{2,1,0:T(8,128)S(1)} %get-tuple-element.206, f32[8]{0:T(128)S(1)} %dynamic-slice_bitcast_fusion.2, pred[]{:T(512)S(6)} %compare.3, pred[]{:T(512)S(6)} %lt.33), kind=kLoop, calls=%fused_computation.1.clone.1 | loop fusion | flops 524288 | bytes 1572902 | tf_op jit(solution)/shard_map/while/body/eval_jaxpr/jit(_where)/select_n | solution.py:23
  79.8 1.2 %fusion.49 = f32[8,128,128]{2,1,0:T(8,128)S(1)} fusion(f32[8,8,128,128]{3,2,1,0:T(8,128)} %get-tuple-element.216, s32[]{:T(128)} %get-tuple-element.205, f32[8,128,128]{2,1,0:T(8,128)S(1)} %get-tuple-element.206, f32[8]{0:T(128)S(1)} %dynamic-slice_bitcast_fusion.2, pred[]{:T(512)S(6)} %compare.3, pred[]{:T(512)S(6)} %lt.33), kind=kLoop, calls=%fused_computation.1.clone.1 | loop fusion | flops 524288 | bytes 1572902 | tf_op jit(solution)/shard_map/while/body/eval_jaxpr/jit(_where)/select_n | solution.py:23
  81.0 1.2 %fusion.49 = f32[8,128,128]{2,1,0:T(8,128)S(1)} fusion(f32[8,8,128,128]{3,2,1,0:T(8,128)} %get-tuple-element.216, s32[]{:T(128)} %get-tuple-element.205, f32[8,128,128]{2,1,0:T(8,128)S(1)} %get-tuple-element.206, f32[8]{0:T(128)S(1)} %dynamic-slice_bitcast_fusion.2, pred[]{:T(512)S(6)} %compare.3, pred[]{:T(512)S(6)} %lt.33), kind=kLoop, calls=%fused_computation.1.clone.1 | loop fusion | flops 524288 | bytes 1572902 | tf_op jit(solution)/shard_map/while/body/eval_jaxpr/jit(_where)/select_n | solution.py:23
  82.2 1.2 %fusion.49 = f32[8,128,128]{2,1,0:T(8,128)S(1)} fusion(f32[8,8,128,128]{3,2,1,0:T(8,128)} %get-tuple-element.216, s32[]{:T(128)} %get-tuple-element.205, f32[8,128,128]{2,1,0:T(8,128)S(1)} %get-tuple-element.206, f32[8]{0:T(128)S(1)} %dynamic-slice_bitcast_fusion.2, pred[]{:T(512)S(6)} %compare.3, pred[]{:T(512)S(6)} %lt.33), kind=kLoop, calls=%fused_computation.1.clone.1 | loop fusion | flops 524288 | bytes 1572902 | tf_op jit(solution)/shard_map/while/body/eval_jaxpr/jit(_where)/select_n | solution.py:23
  (41 shorter events, 7.3 us)
Async XLA Ops:
  7.2 4.4 %copy-start = (bf16[64,1024]{1,0:T(8,128)(2,1)S(1)}, bf16[64,1024]{1,0:T(8,128)(2,1)}, u32[]{:S(2)}) copy-start(bf16[64,1024]{1,0:T(8,128)(2,1)} %param.12) | copy-start | bytes 393220
  7.2 66.6 %all-gather.4.cloned.1.call-start = ((), (), s32[]{:S(2)}) async-start(), calls=%async_computation.3 | async-start | bytes 4718592 | tf_op jit(solution)/shard_map/all_gather | solution.py:13
  15.3 11.9 %all-to-all-start = ((bf16[16,4,128]{2,0,1:T(8,128)(2,1)}), bf16[16,4,128]{2,0,1:T(8,128)(2,1)S(1)}, u32[]{:S(2)}, u32[]{:S(2)}) async-start(bf16[16,4,128]{2,0,1:T(8,128)(2,1)} %copy_bitcast_fusion.4), calls=%async_computation | async-start | bytes 32768 | tf_op jit(solution)/shard_map/all_to_all | solution.py:82
  27.3 20.8 %all-to-all-start.2 = ((bf16[16,4,128]{2,0,1:T(8,128)(2,1)}), bf16[16,4,128]{2,0,1:T(8,128)(2,1)S(1)}, u32[]{:S(2)}, u32[]{:S(2)}) async-start(bf16[16,4,128]{2,0,1:T(8,128)(2,1)} %copy_bitcast_fusion.3), calls=%async_computation.2 | async-start | bytes 32768 | tf_op jit(solution)/shard_map/all_to_all | solution.py:83
  48.1 23.0 %all-to-all-start.1 = ((bf16[16,4,1024]{2,0,1:T(8,128)(2,1)}), bf16[16,4,1024]{2,0,1:T(8,128)(2,1)S(1)}, u32[]{:S(2)}, u32[]{:S(2)}) async-start(bf16[16,4,1024]{2,0,1:T(8,128)(2,1)} %bitcast.137), calls=%async_computation.1 | async-start | bytes 262144 | tf_op jit(solution)/shard_map/all_to_all | solution.py:81
  72.5 11.0 %copy-start.1 = (bf16[64,1024]{1,0:T(8,128)(2,1)S(1)}, bf16[64,1024]{1,0:T(8,128)(2,1)}, u32[]{:S(2)}) copy-start(bf16[64,1024]{1,0:T(8,128)(2,1)} %param.10) | copy-start | bytes 393220
Sparse Core Ops, SparseCore 0:
  14.1 39.5 all-gather.3
where the time goes:
time: 92.9 us; the launch traced here: 91.8 us
  blocking collectives  30 us (32%)
  between operations  15.5 us (17%)
  other arithmetic  15.1 us (16%)
  starting transfers between devices  14.4 us (16%)
  local copies, waits for them, and re-layouts  7.97 us (9%)
  matrix products  5.12 us (6%)
  waiting for transfers between devices  3.56 us (4%)
    unnamed x1, blocking collectives  12.5 us
    select_n x8, other arithmetic, lap(): return jax.tree.map(lambda a, b: jnp.where(reached, a, b), new, before)  9.38 us
    all_gather x1, blocking collectives, softmax_part(): key_piece = lax.all_gather(keys_local, 'seq', axis=0, tiled=True)  9.07 us
    all_gather x1, blocking collectives, softmax_part(): value_piece = lax.all_gather(values_local, 'seq', axis=0, tiled=True)  8.36 us
    all_to_all x1, starting transfers between devices, softmax_part(): lax.all_to_all(key_soft, 'head', split_axis=1, concat_axis=0, tiled=True)  6.32 us
    all_to_all x1, starting transfers between devices, softmax_part(): lax.all_to_all(query_soft, 'head', split_axis=1, concat_axis=0, tiled=True)  4.78 us
    all_to_all x1, waiting for transfers between devices, softmax_part(): lax.all_to_all(key_soft, 'head', split_axis=1, concat_axis=0, tiled=True)  3.54 us
    all_to_all x1, starting transfers between devices, softmax_part(): lax.all_to_all(value_soft, 'head', split_axis=1, concat_axis=0, tiled=True)  3.25 us
  transfers between devices with their start and end apart: 4, of which 1 were waited for; matrix products, arithmetic and copies ran while one was open for 12% of the time, Pallas kernels for 0%

commit v1 on v0

--- a/solution.py
+++ b/solution.py
@@ -94,8 +94,13 @@
         jnp.zeros((span_len, kv_count, group_size), jnp.float32),
         jnp.zeros((span_len, kv_count, group_size, DH), jnp.float32),
     )
-    key_piece = lax.all_gather(keys_local, "seq", axis=0, tiled=True)
-    value_piece = lax.all_gather(values_local, "seq", axis=0, tiled=True)
+    key_piece, value_piece = jnp.split(
+        lax.all_gather(
+            jnp.concatenate([keys_local, values_local], axis=1), axis_name="seq", axis=0, tiled=True
+        ),
+        [keys_local.shape[1]],
+        axis=1,
+    )
     piece_rows = key_piece.shape[0]
     block_rows = max(
         (divisor for divisor in range(1, min(piece_rows, 1024) + 1) if piece_rows % divisor == 0)

time: 92.9 us -> 85.5 us (0.920)
  blocking collectives: 30 us -> 21.3 us
  waiting for transfers between devices: 3.56 us -> 6.39 us
  starting transfers between devices: 14.4 us -> 13 us
    all_gather x2 -> x1, blocking collectives: 17.4 us -> 9.31 us  [softmax_part(): lax.all_gather(jnp.concatenate([keys_local, values_local], axis=1), axis_...]
    all_to_all x1, waiting for transfers between devices: 0.01 us -> 3.54 us  [softmax_part(): lax.all_to_all(value_soft, 'head', split_axis=1, concat_axis=0, tiled=True)]
    all_to_all x1, starting transfers between devices: 6.32 us -> 3.25 us  [softmax_part(): lax.all_to_all(key_soft, 'head', split_axis=1, concat_axis=0, tiled=True)]
    all_to_all x1, starting transfers between devices: 3.25 us -> 6.32 us  [softmax_part(): lax.all_to_all(value_soft, 'head', split_axis=1, concat_axis=0, tiled=True)]
    all_to_all x1, starting transfers between devices: 4.78 us -> 3.34 us  [softmax_part(): lax.all_to_all(query_soft, 'head', split_axis=1, concat_axis=0, tiled=True)]
  transfers between devices with their start and end apart: 4 -> 4, of which waited for: 1 -> 2; matrix products, arithmetic and copies ran while one was open for 12% -> 13% of each run, Pallas kernels for 0% -> 0%
where the time goes in v1:
time: 85.5 us; the launch traced here: 84.5 us
  blocking collectives  21.3 us (25%)
  between operations  15.5 us (18%)
  other arithmetic  15.1 us (18%)
  starting transfers between devices  13 us (15%)
  local copies, waits for them, and re-layouts  7.89 us (9%)
  waiting for transfers between devices  6.39 us (7%)
  matrix products  5.03 us (6%)
    unnamed x1, blocking collectives  12 us
    select_n x8, other arithmetic, lap(): return jax.tree.map(lambda a, b: jnp.where(reached, a, b), new, before)  9.38 us
    all_gather x1, blocking collectives, softmax_part(): lax.all_gather(jnp.concatenate([keys_local, values_local], axis=1), axis_...  9.31 us
    all_to_all x1, starting transfers between devices, softmax_part(): lax.all_to_all(value_soft, 'head', split_axis=1, concat_axis=0, tiled=True)  6.32 us
    all_to_all x1, waiting for transfers between devices, softmax_part(): lax.all_to_all(value_soft, 'head', split_axis=1, concat_axis=0, tiled=True)  3.54 us
    all_to_all x1, starting transfers between devices, softmax_part(): lax.all_to_all(query_soft, 'head', split_axis=1, concat_axis=0, tiled=True)  3.34 us
    all_to_all x1, starting transfers between devices, softmax_part(): lax.all_to_all(key_soft, 'head', split_axis=1, concat_axis=0, tiled=True)  3.25 us
    all_to_all x1, waiting for transfers between devices, softmax_part(): lax.all_to_all(key_soft, 'head', split_axis=1, concat_axis=0, tiled=True)  2.83 us
  transfers between devices with their start and end apart: 4, of which 2 were waited for; matrix products, arithmetic and copies ran while one was open for 13% of the time, Pallas kernels for 0%

profile of v1, /device:TPU:0, one launch (start us, length us, event | category | flops | bytes accessed | tf_op | source)
XLA Modules:
  0.0 84.5 jit_solution(9442633476704783729)
XLA Ops:
  7.2 1.2 %slice.8 = s32[1]{0:T(128)} slice(s32[64]{0:T(128)} %param.17), slice={[63:64]} | slice | bytes 8 | tf_op jit(solution)/shard_map/slice | solution.py:46
  9.1 1.3 %compare_convert_fusion = (f32[64]{0:T(128)S(1)}, f32[64]{0:T(128)S(1)}) fusion(s32[64]{0:T(128)} %param.17, s32[]{:T(128)S(6)} %mul.138, s32[]{:T(128)} %bitcast.1), kind=kLoop, calls=%fused_computation.68 | loop fusion | flops 256 | bytes 776 | tf_op jit(solution)/shard_map/convert_element_type | solution.py:48
  11.6 2.4 %fusion.15 = f32[8,128,128]{2,1,0:T(8,128)} fusion(f32[64,8]{0,1:T(8,128)S(1)} %get-tuple-element.158, bf16[64,1024]{1,0:T(8,128)(2,1)S(1)} %copy-done, bf16[64,1024]{1,0:T(8,128)(2,1)} %param.11), kind=kOutput, calls=%fused_computation.25 | convolution fusion | flops 100794368 | bytes 788480 | tf_op jit(solution)/shard_map/shd,she->hde/dot_general | solution.py:45
  14.0 1.3 %copy_bitcast_fusion.3 = bf16[16,4,128]{2,0,1:T(8,128)(2,1)} fusion(bf16[16,512]{1,0:T(8,128)(2,1)} %param.16), kind=kLoop, calls=%fused_computation.53 | loop fusion | bytes 32768 | tf_op jit(solution)/shard_map/all_to_all | solution.py:83
  15.3 6.3 %all-to-all-start.1 = ((bf16[16,4,128]{2,0,1:T(8,128)(2,1)}), bf16[16,4,128]{2,0,1:T(8,128)(2,1)S(1)}, u32[]{:S(2)}, u32[]{:S(2)}) async-start(bf16[16,4,128]{2,0,1:T(8,128)(2,1)} %copy_bitcast_fusion.3), calls=%async_computation.1 | async-start | bytes 32768 | tf_op jit(solution)/shard_map/all_to_all | solution.py:83
  21.7 1.3 %copy_bitcast_fusion.4 = bf16[16,4,128]{2,0,1:T(8,128)(2,1)} fusion(bf16[16,512]{1,0:T(8,128)(2,1)} %param.15), kind=kLoop, calls=%fused_computation.54 | loop fusion | bytes 32768 | tf_op jit(solution)/shard_map/all_to_all | solution.py:82
  23.7 3.5 %all-to-all-done.1 = bf16[16,4,128]{2,0,1:T(8,128)(2,1)S(1)} async-done(((bf16[16,4,128]{2,0,1:T(8,128)(2,1)}), bf16[16,4,128]{2,0,1:T(8,128)(2,1)S(1)}, u32[]{:S(2)}, u32[]{:S(2)}) %all-to-all-start.1) | async-done | bytes 16416 | tf_op jit(solution)/shard_map/all_to_all | solution.py:83
  27.3 3.3 %all-to-all-start = ((bf16[16,4,128]{2,0,1:T(8,128)(2,1)}), bf16[16,4,128]{2,0,1:T(8,128)(2,1)S(1)}, u32[]{:S(2)}, u32[]{:S(2)}) async-start(bf16[16,4,128]{2,0,1:T(8,128)(2,1)} %copy_bitcast_fusion.4), calls=%async_computation | async-start | bytes 32768 | tf_op jit(solution)/shard_map/all_to_all | solution.py:82
  30.5 1.2 %convolution_multiply_fusion.1 = f32[8,64,64]{2,1,0:T(8,128)S(1)} fusion(f32[8,64]{1,0:T(8,128)S(1)} %reduce_window_sum.11, pred[64,64]{1,0:T(8,128)(4,1)S(1)} %compare_and_fusion, bf16[64,1024]{1,0:T(8,128)(2,1)} %param.11, bf16[64,1024]{1,0:T(8,128)(2,1)} %param.10), kind=kOutput, calls=%fused_computation.11 | convolution fusion | flops 8519680 | bytes 399360 | tf_op jit(solution)/shard_map/thd,shd->hts/dot_general | solution.py:38
  31.7 1.6 %copy.84 = bf16[2,4,8,1024]{3,2,0,1:T(8,128)(2,1)} copy(bf16[2,4,8,1024]{3,2,1,0:T(8,128)(2,1)} %bitcast.148) | data formatting | bytes 262144 | tf_op jit(solution)/shard_map/all_to_all | solution.py:81
  33.3 2.8 %all-to-all-done = bf16[16,4,128]{2,0,1:T(8,128)(2,1)S(1)} async-done(((bf16[16,4,128]{2,0,1:T(8,128)(2,1)}), bf16[16,4,128]{2,0,1:T(8,128)(2,1)S(1)}, u32[]{:S(2)}, u32[]{:S(2)}) %all-to-all-start) | async-done | bytes 16416 | tf_op jit(solution)/shard_map/all_to_all | solution.py:82
  36.1 3.3 %all-to-all-start.2 = ((bf16[16,4,1024]{2,0,1:T(8,128)(2,1)}), bf16[16,4,1024]{2,0,1:T(8,128)(2,1)S(1)}, u32[]{:S(2)}, u32[]{:S(2)}) async-start(bf16[16,4,1024]{2,0,1:T(8,128)(2,1)} %bitcast.139), calls=%async_computation.2 | async-start | bytes 262144 | tf_op jit(solution)/shard_map/all_to_all | solution.py:81
  40.2 1.2 %dynamic-slice = u32[1]{0:T(128)} dynamic-slice(u32[32]{0:T(128)} %constant.72, u32[]{:T(128)S(6)} %add.102), dynamic_slice_sizes={1} | dynamic-slice | bytes 12
  42.4 12.0 %all-reduce = f32[64]{0:T(128)S(1)} all-reduce(f32[64]{0:T(128)S(1)} %dynamic-update-slice), channel_id=2, replica_groups=mesh['seq'=8,'head'=4] {'seq'}, use_global_device_ids=true, to_apply=%add | all-reduce | flops 64 | bytes 512
  54.5 9.3 %all_gather.16 = bf16[512,256]{1,0:T(8,128)(2,1)S(1)} all-gather(bf16[64,256]{1,0:T(8,128)(2,1)S(1)} %pad_maximum_fusion), channel_id=1, replica_groups=mesh['seq'=8,'head'=4] {'seq'}, dimensions={0}, use_global_device_ids=true | all-gather | bytes 294912 | tf_op jit(solution)/shard_map/all_gather | solution.py:98
  66.4 9.7 %while.9 = (s32[]{:T(128)}, f32[8,128,128]{2,1,0:T(8,128)S(1)}, s32[]{:T(128)}, f32[8,8]{1,0:T(8,128)S(1)}, f32[8,8,128,128]{3,2,1,0:T(8,128)}, /*index=5*/s32[]{:T(128)}, s32[]{:T(128)}) while((s32[]{:T(128)}, f32[8,128,128]{2,1,0:T(8,128)S(1)}, s32[]{:T(128)}, f32[8,8]{1,0:T(8,128)S(1)}, f32[8,8,128,128]{3,2,1,0:T(8,128)}, ...), condition=%wide.region_2.3_spmd.clone, body=%wide.region_1.2_spmd.clone.sunk | while | flops 524292 | bytes 1573073 | solution.py:25
  66.4 1.2 %fusion.52 = f32[8,128,128]{2,1,0:T(8,128)S(1)} fusion(f32[8,8,128,128]{3,2,1,0:T(8,128)} %get-tuple-element.214, s32[]{:T(128)S(6)} %copy.88, f32[8,128,128]{2,1,0:T(8,128)S(1)} %get-tuple-element.204, f32[8]{0:T(128)S(1)} %dynamic-slice_bitcast_fusion.2, pred[]{:T(512)S(6)} %compare.3, pred[]{:T(512)S(6)} %lt.33), kind=kLoop, calls=%fused_computation.1.clone.1 | loop fusion | flops 524288 | bytes 1572902 | tf_op jit(solution)/shard_map/while/body/eval_jaxpr/jit(_where)/select_n | solution.py:23
  67.6 1.2 %fusion.52 = f32[8,128,128]{2,1,0:T(8,128)S(1)} fusion(f32[8,8,128,128]{3,2,1,0:T(8,128)} %get-tuple-element.214, s32[]{:T(128)S(6)} %copy.88, f32[8,128,128]{2,1,0:T(8,128)S(1)} %get-tuple-element.204, f32[8]{0:T(128)S(1)} %dynamic-slice_bitcast_fusion.2, pred[]{:T(512)S(6)} %compare.3, pred[]{:T(512)S(6)} %lt.33), kind=kLoop, calls=%fused_computation.1.clone.1 | loop fusion | flops 524288 | bytes 1572902 | tf_op jit(solution)/shard_map/while/body/eval_jaxpr/jit(_where)/select_n | solution.py:23
  68.8 1.2 %fusion.52 = f32[8,128,128]{2,1,0:T(8,128)S(1)} fusion(f32[8,8,128,128]{3,2,1,0:T(8,128)} %get-tuple-element.214, s32[]{:T(128)S(6)} %copy.88, f32[8,128,128]{2,1,0:T(8,128)S(1)} %get-tuple-element.204, f32[8]{0:T(128)S(1)} %dynamic-slice_bitcast_fusion.2, pred[]{:T(512)S(6)} %compare.3, pred[]{:T(512)S(6)} %lt.33), kind=kLoop, calls=%fused_computation.1.clone.1 | loop fusion | flops 524288 | bytes 1572902 | tf_op jit(solution)/shard_map/while/body/eval_jaxpr/jit(_where)/select_n | solution.py:23
  70.0 1.2 %fusion.52 = f32[8,128,128]{2,1,0:T(8,128)S(1)} fusion(f32[8,8,128,128]{3,2,1,0:T(8,128)} %get-tuple-element.214, s32[]{:T(128)S(6)} %copy.88, f32[8,128,128]{2,1,0:T(8,128)S(1)} %get-tuple-element.204, f32[8]{0:T(128)S(1)} %dynamic-slice_bitcast_fusion.2, pred[]{:T(512)S(6)} %compare.3, pred[]{:T(512)S(6)} %lt.33), kind=kLoop, calls=%fused_computation.1.clone.1 | loop fusion | flops 524288 | bytes 1572902 | tf_op jit(solution)/shard_map/while/body/eval_jaxpr/jit(_where)/select_n | solution.py:23
  71.2 1.2 %fusion.52 = f32[8,128,128]{2,1,0:T(8,128)S(1)} fusion(f32[8,8,128,128]{3,2,1,0:T(8,128)} %get-tuple-element.214, s32[]{:T(128)S(6)} %copy.88, f32[8,128,128]{2,1,0:T(8,128)S(1)} %get-tuple-element.204, f32[8]{0:T(128)S(1)} %dynamic-slice_bitcast_fusion.2, pred[]{:T(512)S(6)} %compare.3, pred[]{:T(512)S(6)} %lt.33), kind=kLoop, calls=%fused_computation.1.clone.1 | loop fusion | flops 524288 | bytes 1572902 | tf_op jit(solution)/shard_map/while/body/eval_jaxpr/jit(_where)/select_n | solution.py:23
  72.5 1.2 %fusion.52 = f32[8,128,128]{2,1,0:T(8,128)S(1)} fusion(f32[8,8,128,128]{3,2,1,0:T(8,128)} %get-tuple-element.214, s32[]{:T(128)S(6)} %copy.88, f32[8,128,128]{2,1,0:T(8,128)S(1)} %get-tuple-element.204, f32[8]{0:T(128)S(1)} %dynamic-slice_bitcast_fusion.2, pred[]{:T(512)S(6)} %compare.3, pred[]{:T(512)S(6)} %lt.33), kind=kLoop, calls=%fused_computation.1.clone.1 | loop fusion | flops 524288 | bytes 1572902 | tf_op jit(solution)/shard_map/while/body/eval_jaxpr/jit(_where)/select_n | solution.py:23
  73.7 1.2 %fusion.52 = f32[8,128,128]{2,1,0:T(8,128)S(1)} fusion(f32[8,8,128,128]{3,2,1,0:T(8,128)} %get-tuple-element.214, s32[]{:T(128)S(6)} %copy.88, f32[8,128,128]{2,1,0:T(8,128)S(1)} %get-tuple-element.204, f32[8]{0:T(128)S(1)} %dynamic-slice_bitcast_fusion.2, pred[]{:T(512)S(6)} %compare.3, pred[]{:T(512)S(6)} %lt.33), kind=kLoop, calls=%fused_computation.1.clone.1 | loop fusion | flops 524288 | bytes 1572902 | tf_op jit(solution)/shard_map/while/body/eval_jaxpr/jit(_where)/select_n | solution.py:23
  74.9 1.2 %fusion.52 = f32[8,128,128]{2,1,0:T(8,128)S(1)} fusion(f32[8,8,128,128]{3,2,1,0:T(8,128)} %get-tuple-element.214, s32[]{:T(128)S(6)} %copy.88, f32[8,128,128]{2,1,0:T(8,128)S(1)} %get-tuple-element.204, f32[8]{0:T(128)S(1)} %dynamic-slice_bitcast_fusion.2, pred[]{:T(512)S(6)} %compare.3, pred[]{:T(512)S(6)} %lt.33), kind=kLoop, calls=%fused_computation.1.clone.1 | loop fusion | flops 524288 | bytes 1572902 | tf_op jit(solution)/shard_map/while/body/eval_jaxpr/jit(_where)/select_n | solution.py:23
  (40 shorter events, 7.2 us)
Async XLA Ops:
  7.2 4.4 %copy-start = (bf16[64,1024]{1,0:T(8,128)(2,1)S(1)}, bf16[64,1024]{1,0:T(8,128)(2,1)}, u32[]{:S(2)}) copy-start(bf16[64,1024]{1,0:T(8,128)(2,1)} %param.12) | copy-start | bytes 393220
  7.2 59.2 %all-gather.4.cloned.1.call-start = ((), (), s32[]{:S(2)}) async-start(), calls=%async_computation.3 | async-start | bytes 4718592 | tf_op jit(solution)/shard_map/all_gather | solution.py:13
  15.3 11.9 %all-to-all-start.1 = ((bf16[16,4,128]{2,0,1:T(8,128)(2,1)}), bf16[16,4,128]{2,0,1:T(8,128)(2,1)S(1)}, u32[]{:S(2)}, u32[]{:S(2)}) async-start(bf16[16,4,128]{2,0,1:T(8,128)(2,1)} %copy_bitcast_fusion.3), calls=%async_computation.1 | async-start | bytes 32768 | tf_op jit(solution)/shard_map/all_to_all | solution.py:83
  27.3 8.8 %all-to-all-start = ((bf16[16,4,128]{2,0,1:T(8,128)(2,1)}), bf16[16,4,128]{2,0,1:T(8,128)(2,1)S(1)}, u32[]{:S(2)}, u32[]{:S(2)}) async-start(bf16[16,4,128]{2,0,1:T(8,128)(2,1)} %copy_bitcast_fusion.4), calls=%async_computation | async-start | bytes 32768 | tf_op jit(solution)/shard_map/all_to_all | solution.py:82
  36.1 27.7 %all-to-all-start.2 = ((bf16[16,4,1024]{2,0,1:T(8,128)(2,1)}), bf16[16,4,1024]{2,0,1:T(8,128)(2,1)S(1)}, u32[]{:S(2)}, u32[]{:S(2)}) async-start(bf16[16,4,1024]{2,0,1:T(8,128)(2,1)} %bitcast.139), calls=%async_computation.2 | async-start | bytes 262144 | tf_op jit(solution)/shard_map/all_to_all | solution.py:81
  65.1 11.0 %copy-start.1 = (bf16[64,1024]{1,0:T(8,128)(2,1)S(1)}, bf16[64,1024]{1,0:T(8,128)(2,1)}, u32[]{:S(2)}) copy-start(bf16[64,1024]{1,0:T(8,128)(2,1)} %param.10) | copy-start | bytes 393220
Sparse Core Ops, SparseCore 0:
  14.1 39.4 all-gather.3
